TPU v7x, 128 devices: a whole 4x4x4 slice. The times are simulated.
128 devices in a mesh: inp: 32 (over y_hi, x, z), tm: 4 (over y_lo, core).
Axes of the slice: x: 4, y: 4 (y_hi: 2, y_lo: 2; y = y_hi * 2 + y_lo), z: 4, core: 2. Of those that a mesh axis runs over, the one named last changes fastest.
Arguments:
- voltages: float32 [256, 256, 2048], P('inp', 'tm'), may hold values from -6 to 6
- filter_taps: float32 [4, 2048], replicated, may hold values from -1 to 2
Outputs:
- visibilities: float32 [2, 1024, 256, 256], P(None, ('inp', 'tm'))
All inputs are finite; a program needn't handle non-finite values.
Results may differ from a plain program's by a relative error of at most 0.000084.
Values sent between devices are 32-bit elements; how exact they have to be, the bound alone decides.
A program may use at most 128 MiB of HBM per device.

v0:
```python
import math

import jax
import jax.numpy as jnp
from jax import lax
from jax.sharding import PartitionSpec as P


def from_behind(value, axis, steps):
    count = lax.axis_size(axis)
    leading, last = (max(0, -steps), min(count, count - steps))
    return lax.ppermute(value, axis, [(source, source + steps) for source in range(leading, last)])


def transform_table(nfft, half):
    channel = jnp.arange(half, dtype=jnp.int32)
    sample = jnp.arange(nfft, dtype=jnp.int32)
    phase = channel[:, None] * sample[None, :] % nfft
    angle = 2.0 * math.pi / nfft * phase.astype(jnp.float32)
    scale = 1.0 / math.sqrt(nfft)
    return jnp.concatenate([jnp.cos(angle), -jnp.sin(angle)], axis=0) * scale


def correlate_pair(rows, cols):
    return jnp.einsum("cas,cbs->cab", rows, cols, precision=lax.Precision.HIGHEST)


def on_device(voltages, filter_taps):
    inputs_dev = voltages.shape[0]
    frames_dev = voltages.shape[1]
    nfft = voltages.shape[2]
    taps = filter_taps.shape[0]
    half = nfft // 2
    history = from_behind(voltages[:, frames_dev - (taps - 1) :, :], "tm", 1)
    extended = jnp.concatenate([history, voltages], axis=1)
    filtered = filter_taps[0] * extended[:, 0:frames_dev, :]
    for k in range(1, taps):
        filtered = filtered + filter_taps[k] * extended[:, k : k + frames_dev, :]
    table = transform_table(nfft, half)
    spectra = jnp.einsum("kn,ifn->kif", table, filtered, precision=lax.Precision.HIGHEST)
    spectra = spectra.reshape(2, half, inputs_dev, frames_dev)
    mixed = lax.all_to_all(spectra, ("inp", "tm"), split_axis=1, concat_axis=2, tiled=True)
    n_inp = lax.axis_size("inp")
    n_tm = lax.axis_size("tm")
    owned_ch = mixed.shape[1]
    mixed = mixed.reshape(2, owned_ch, n_inp, n_tm, inputs_dev, frames_dev)
    mixed = jnp.transpose(mixed, (0, 1, 2, 4, 3, 5))
    owned = mixed.reshape(2, owned_ch, n_inp * inputs_dev, n_tm * frames_dev)
    spec_re = owned[0]
    spec_im = owned[1]
    spectra_all = spec_re.shape[2]
    plain = jnp.concatenate([spec_re, spec_im], axis=-1)
    turned = jnp.concatenate([spec_im, -spec_re], axis=-1)
    real_part = correlate_pair(plain, plain)
    imag_part = correlate_pair(turned, plain)
    return jnp.stack([real_part, imag_part]) / spectra_all


def solution(mesh):
    placed = (P("inp", "tm", None), P())
    return jax.shard_map(
        on_device,
        mesh=mesh,
        in_specs=placed,
        out_specs=P(None, ("inp", "tm"), None, None),
        check_vma=False,
    )
```

profile of v0, /device:TPU:1, one launch (start us, length us, event | category | flops | bytes accessed | tf_op | source)
XLA Modules:
  0.0 227.3 jit_solution(11571592242906335460)
XLA Ops:
  0.0 1.1 slice.33
  1.1 0.0 copy-start.3
  1.1 0.0 copy-start.4
  1.1 4.9 %collective-permute-start = (f32[8,3,2048]{2,1,0:T(4,128)S(1)}, f32[8,3,2048]{2,1,0:T(4,128)S(1)}, u32[]{:S(2)}, u32[]{:S(2)}) collective-permute-start(f32[8,3,2048]{2,1,0:T(4,128)S(1)} %slice.33), channel_id=1, source_target_pairs={{0,1},{1,2},{2,3},{4,5},{5,6},{6,7},{8,9},{9,10},{10,11},{12,13},{... | collective-permute-start | bytes 589832 | tf_op jit(solution)/shard_map/ppermute | solution.py:12
  6.0 32.9 %sine_negate_fusion = (f32[1024,2048]{1,0:T(8,128)S(1)}, f32[1024,2048]{1,0:T(8,128)S(1)}) fusion(), kind=kLoop, calls=%fused_computation.12 | loop fusion | flops 31457280 | bytes 16777216 | tf_op jit(solution)/shard_map/neg | solution.py:21
  38.9 0.0 copy-done.3
  38.9 0.0 collective-permute-done
  38.9 0.0 copy-done.4
  38.9 32.5 %fusion.1 = f32[2048,8,64]{0,2,1:T(8,128)} fusion(f32[1024,2048]{1,0:T(8,128)S(1)} %get-tuple-element.13, f32[1024,2048]{1,0:T(8,128)S(1)} %get-tuple-element.14, f32[8,64,2048]{2,1,0:T(8,128)S(1)} %copy-done.4, f32[8,3,2048]{2,1,0:T(4,128)S(1)} %collective-permute-done, f32[2048]{0:T(1024)S(1)} %bitcast.29, f32[2048]{0:T(1024)S(1)} %bitcast.30, ...), kind=kOutput, calls=%fused_computation.2 | convolution fusion | flops 25788678144 | bytes 25395200 | tf_op jit(solution)/shard_map/kn,ifn->kif/dot_general | solution.py:40
  71.4 6.6 %reshape.16 = f32[2,1024,8,64]{1,0,3,2:T(2,128)} reshape(f32[2048,8,64]{0,2,1:T(8,128)} %fusion.1) | data formatting | bytes 8388608 | tf_op jit(solution)/shard_map/reshape | solution.py:41
  78.0 8.6 %copy.7 = f32[2,1024,8,64]{3,2,0,1:T(8,128)} copy(f32[2,1024,8,64]{1,0,3,2:T(2,128)} %reshape.16) | data formatting | bytes 8388608 | tf_op jit(solution)/shard_map/reshape | solution.py:41
  86.6 9.4 %reshape.19 = f32[128,1,8192]{2,1,0:T(1,128)} reshape(f32[1024,2,8,64]{3,2,1,0:T(8,128)} %bitcast.24) | data formatting | bytes 8388608
  96.0 63.1 %all_to_all.15 = f32[128,1,8192]{2,1,0:T(1,128)} all-to-all(f32[128,1,8192]{2,1,0:T(1,128)} %reshape.19), channel_id=1, replica_groups=mesh['inp'=32,'tm'=4] {'inp','tm'}, dimensions={0} | all-to-all | bytes 8388608 | tf_op jit(solution)/shard_map/all_to_all | solution.py:42
  159.1 0.5 broadcast.13
  159.6 13.8 %reduce = f32[128,8192]{1,0:T(8,128)} reduce(f32[128,1,8192]{2,1,0:T(1,128)} %all_to_all.15, f32[]{:T(128)} %broadcast.13), dimensions={1}, to_apply=%all_to_all.11.reduce_sub_computation | reduce | bytes 8388612 | tf_op jit(solution)/shard_map/all_to_all | solution.py:42
  173.5 7.9 %reshape.20 = f32[1024,2,8,64]{3,2,1,0:T(8,128)} reshape(f32[128,8192]{1,0:T(8,128)} %reduce) | data formatting | bytes 8388608
  181.3 4.2 %copy.9 = f32[2,8,128,8,64]{4,3,2,1,0:T(8,128)S(1)} copy(f32[2,8,128,8,64]{4,3,0,1,2:T(8,128)} %bitcast.26) | data formatting | bytes 8388608 | tf_op jit(solution)/shard_map/all_to_all | solution.py:42
  185.6 3.0 %fusion.40 = (f32[1,8,32,8,4,64]{5,3,4,2,1,0:T(8,128)}, f32[1,8,32,8,4,64]{5,3,4,2,1,0:T(8,128)S(1)}) fusion(f32[2,8,32,8,4,64]{5,3,4,2,1,0:T(8,128)S(1)} %bitcast.25), kind=kLoop, calls=%fused_computation.48 | loop fusion | bytes 8388608 | tf_op jit(solution)/shard_map/slice | solution.py:50
  188.6 3.3 %copy.10 = f32[1,8,32,8,4,64]{5,4,3,2,1,0:T(4,128)} copy(f32[1,8,32,8,4,64]{5,3,4,2,1,0:T(8,128)S(1)} %get-tuple-element.6) | data formatting | bytes 4194304 | tf_op jit(solution)/shard_map/slice | solution.py:49
  191.9 4.2 %squeeze.6 = f32[8,256,256]{2,1,0:T(8,128)S(1)} reshape(f32[1,8,32,8,4,64]{5,4,3,2,1,0:T(4,128)} %copy.10) | data formatting | bytes 4194304 | tf_op jit(solution)/shard_map/squeeze | solution.py:49
  196.1 0.0 copy-start.1
  196.1 2.5 %fusion.41 = (f32[8,256,256]{2,1,0:T(8,128)}, f32[8,256,512]{2,1,0:T(8,128)}) fusion(f32[8,256,256]{2,1,0:T(8,128)S(1)} %squeeze.6), kind=kLoop, calls=%fused_computation.49 | loop fusion | flops 524287 | bytes 6291456 | tf_op jit(solution)/shard_map/neg | solution.py:53
  198.6 1.2 copy-done.1
  199.8 3.3 %copy.11 = f32[1,8,32,8,4,64]{5,4,3,2,1,0:T(4,128)} copy(f32[1,8,32,8,4,64]{5,3,4,2,1,0:T(8,128)S(1)} %copy-done.1) | data formatting | bytes 4194304 | tf_op jit(solution)/shard_map/slice | solution.py:50
  203.1 4.2 %squeeze.7 = f32[8,256,256]{2,1,0:T(8,128)S(1)} reshape(f32[1,8,32,8,4,64]{5,4,3,2,1,0:T(4,128)} %copy.11) | data formatting | bytes 4194304 | tf_op jit(solution)/shard_map/squeeze | solution.py:50
  207.2 1.7 constant_dynamic-update-slice_fusion
  208.9 0.0 copy-start
  208.9 11.9 %convolution_bitcast_fusion = f32[1,8,256,256]{3,2,1,0:T(8,128)S(1)} fusion(f32[8,256,512]{2,1,0:T(8,128)} %constant_dynamic-update-slice_fusion), kind=kOutput, calls=%fused_computation.42 | convolution fusion | flops 3221225472 | bytes 6291456 | tf_op jit(solution)/shard_map/cas,cbs->cab/dot_general | solution.py:25
  220.8 0.0 copy-done
  220.8 0.0 copy-done.2
  220.8 4.2 %fusion.34 = f32[1,8,256,256]{3,2,1,0:T(8,128)S(1)} fusion(f32[8,256,512]{2,1,0:T(8,128)S(1)} %copy-done, f32[8,256,256]{2,1,0:T(8,128)S(1)} %copy-done.2, f32[8,256,256]{2,1,0:T(8,128)S(1)} %squeeze.7), kind=kOutput, calls=%fused_computation.41 | convolution fusion | flops 3222274048 | bytes 10485760 | tf_op jit(solution)/shard_map/cas,cbs->cab/dot_general | solution.py:25
  225.0 2.3 %maximum_multiply_fusion.1 = f32[2,8,256,256]{3,2,1,0:T(8,128)} fusion(f32[1,8,256,256]{3,2,1,0:T(8,128)S(1)} %fusion.34, f32[1,8,256,256]{3,2,1,0:T(8,128)S(1)} %convolution_bitcast_fusion), kind=kLoop, calls=%fused_computation.34 | loop fusion | flops 2097152 | bytes 8388608 | tf_op jit(solution)/shard_map/div | solution.py:56
  (2 shorter events, 0.0 us)
Async XLA Ops:
  1.1 37.8 %copy-start.3 = (f32[4,2048]{1,0:T(4,128)S(1)}, f32[4,2048]{1,0:T(4,128)}, u32[]{:S(2)}) copy-start(f32[4,2048]{1,0:T(4,128)} %param.3) | copy-start | bytes 98308
  1.1 37.8 %copy-start.4 = (f32[8,64,2048]{2,1,0:T(8,128)S(1)}, f32[8,64,2048]{2,1,0:T(8,128)}, u32[]{:S(2)}) copy-start(f32[8,64,2048]{2,1,0:T(8,128)} %param.2) | copy-start | bytes 12582916
  1.1 37.8 %collective-permute-start = (f32[8,3,2048]{2,1,0:T(4,128)S(1)}, f32[8,3,2048]{2,1,0:T(4,128)S(1)}, u32[]{:S(2)}, u32[]{:S(2)}) collective-permute-start(f32[8,3,2048]{2,1,0:T(4,128)S(1)} %slice.33), channel_id=1, source_target_pairs={{0,1},{1,2},{2,3},{4,5},{5,6},{6,7},{8,9},{9,10},{10,11},{12,13},{... | collective-permute-start | bytes 589832 | tf_op jit(solution)/shard_map/ppermute | solution.py:12
  196.1 3.7 %copy-start.1 = (f32[1,8,32,8,4,64]{5,3,4,2,1,0:T(8,128)S(1)}, f32[1,8,32,8,4,64]{5,3,4,2,1,0:T(8,128)}, u32[]{:S(2)}) copy-start(f32[1,8,32,8,4,64]{5,3,4,2,1,0:T(8,128)} %get-tuple-element.5) | copy-start | bytes 6291460
  208.9 11.9 %copy-start = (f32[8,256,512]{2,1,0:T(8,128)S(1)}, f32[8,256,512]{2,1,0:T(8,128)}, u32[]{:S(2)}) copy-start(f32[8,256,512]{2,1,0:T(8,128)} %constant_dynamic-update-slice_fusion) | copy-start | bytes 12582916
  208.9 11.9 %copy-start.2 = (f32[8,256,256]{2,1,0:T(8,128)S(1)}, f32[8,256,256]{2,1,0:T(8,128)}, u32[]{:S(2)}) copy-start(f32[8,256,256]{2,1,0:T(8,128)} %get-tuple-element.7) | copy-start | bytes 6291460
where the time goes:
time: 230 us; the launch traced here: 227 us
  blocking collectives  63.1 us (27%)
  local copies, waits for them, and re-layouts  59.1 us (26%)
  other arithmetic  51.5 us (22%)
  matrix products  48.5 us (21%)
  starting transfers between devices  4.86 us (2%)
    all_to_all x1, blocking collectives, on_device(): lax.all_to_all(spectra, ('inp', 'tm'), split_axis=1, concat_axis=2, tiled...  63.1 us
    neg x1, other arithmetic, transform_table(): return jnp.concatenate([jnp.cos(angle), -jnp.sin(angle)], axis=0) * scale  32.9 us
    dot_general x1, matrix products, on_device(): jnp.einsum('kn,ifn->kif', table, filtered, precision=lax.Precision.HIGHEST)  32.5 us
    unnamed x12, local copies, waits for them, and re-layouts  18.5 us
    dot_general x2, matrix products, correlate_pair(): jnp.einsum('cas,cbs->cab', rows, cols, precision=lax.Precision.HIGHEST)  16 us
    reshape x2, local copies, waits for them, and re-layouts, on_device(): spectra = spectra.reshape(2, half, inputs_dev, frames_dev)  15.2 us
    all_to_all x1, other arithmetic, on_device(): lax.all_to_all(spectra, ('inp', 'tm'), split_axis=1, concat_axis=2, tiled...  13.8 us
    slice x2, local copies, waits for them, and re-layouts, on_device(): spec_im = owned[1]  6.33 us
  transfers between devices with their start and end apart: 1, of which 0 were waited for; matrix products, arithmetic and copies ran while one was open for 14% of the time, Pallas kernels for 0%

commit v1 on v0

v1 whole, which is shorter than its diff:
```python
import functools
import math

import jax
import jax.numpy as jnp
import numpy as np
from jax import lax
from jax.experimental import pallas as pl
from jax.experimental.pallas import tpu as pltpu
from jax.sharding import PartitionSpec as P

LANES = 128
F32 = jnp.float32
BF16 = jnp.bfloat16


def tables(nfft, spectra):
    dests = 128
    n2 = np.arange(LANES)
    scale = 1.0 / math.sqrt(nfft) / math.sqrt(spectra)
    out = np.zeros((9, dests, 2 * LANES), np.float64)
    for r in range(9):
        for m in range(dests):
            if (r == 0 and m % 2 == 1) or (r == 8 and m % 2 == 0):
                continue
            q = m // 2 if (m % 2 == 0 or r == 8) else 127 - m // 2
            angle = 2.0 * np.pi * ((n2 * (16 * q + r)) % nfft) / nfft
            out[r, m, :LANES] = np.cos(angle) * scale
            out[r, m, LANES:] = np.sin(angle) * scale
    out = out.astype(np.float32)
    high = out.astype(jnp.bfloat16)
    low = (out - high.astype(np.float32)).astype(jnp.bfloat16)
    return np.concatenate([high, low], axis=1)


def split(value):
    high = value.astype(BF16)
    return high, (value - high.astype(F32)).astype(BF16)


def sixteen(x):
    c1, c2, c3 = (math.cos(k * math.pi / 8) for k in (1, 2, 3))
    a = [x[n] + x[n + 8] for n in range(8)]
    b = [x[n] - x[n + 8] for n in range(8)]
    c = [a[n] + a[n + 4] for n in range(4)]
    d = [a[n] - a[n + 4] for n in range(4)]
    c02, c13 = c[0] + c[2], c[1] + c[3]
    y = {0: (c02 + c13, None), 8: (c02 - c13, None), 4: (c[0] - c[2], c[3] - c[1])}
    dm, dp = (d[1] - d[3]) * c2, (d[1] + d[3]) * c2
    y[2] = (d[0] + dm, -(d[2] + dp))
    y[6] = (d[0] - dm, d[2] - dp)
    e = [None] + [b[n] - b[8 - n] for n in (1, 2, 3)]
    g = [None] + [b[n] + b[8 - n] for n in (1, 2, 3)]
    e2, g2 = e[2] * c2, g[2] * c2
    p, q = b[0] + e2, b[0] - e2
    s, t = e[1] * c1 + e[3] * c3, e[1] * c3 - e[3] * c1
    v, w = b[4] + g2, g2 - b[4]
    h, k = g[1] * c3 + g[3] * c1, g[1] * c1 - g[3] * c3
    y[1] = (p + s, -(v + h))
    y[7] = (p - s, v - h)
    y[3] = (q + t, -(k + w))
    y[5] = (q - t, w - k)
    return y


def contract(a, b):
    return lax.dot_general(a, b, (((1,), (1,)), ((), ())), preferred_element_type=F32)


def front_kernel(volt, halo, taps, table, send, ext, tapb, xs, sem):
    inputs, frames = volt.shape[0], volt.shape[1]
    blocks = volt.shape[2] // LANES
    copies = []
    for l in range(blocks):
        lanes = pl.ds(l * LANES, LANES)
        copies.append(pltpu.make_async_copy(volt.at[:, :, lanes], ext.at[:, l, pl.ds(8, frames), :], sem.at[l]))
        copies[-1].start()
    for k in range(4):
        for l in range(blocks):
            tapb[k, l] = jnp.broadcast_to(taps[k : k + 1, l * LANES : (l + 1) * LANES], (8, LANES))
    for i in range(inputs):
        for l in range(blocks):
            ext[i, l, 5:8, :] = halo[i, :, l * LANES : (l + 1) * LANES]
    for copy in copies:
        copy.wait()

    step = 16

    @pl.loop(0, inputs)
    def _(i):
        for f in range(frames // step):
            parts = []
            for l in range(blocks):
                halves = []
                for j in range(step // 8):
                    row = 5 + f * step + j * 8
                    acc = tapb[0, l] * ext[i, l, pl.ds(row, 8), :]
                    for k in range(1, 4):
                        acc = acc + tapb[k, l] * ext[i, l, pl.ds(row + k, 8), :]
                    halves.append(acc)
                parts.append(jnp.concatenate(halves, axis=0))
            y = sixteen(parts)
            rows = pl.ds(pl.multiple_of(i * frames, frames) + f * step, step)
            for r in range(9):
                real, imag = y[r]
                high, low = split(real)
                xs[r, 0, 0, rows, :] = high
                xs[r, 1, 0, rows, :] = low
                xs[r, 0, 1, rows, :] = -high
                xs[r, 1, 1, rows, :] = -low
                if imag is not None:
                    high, low = split(imag)
                    xs[r, 0, 2, rows, :] = high
                    xs[r, 1, 2, rows, :] = low

    def operand(r, part, pair):
        blocks_ = []
        for i in (2 * pair, 2 * pair + 1):
            rows = pl.ds(i * frames, frames)
            real, minus = xs[r, part, 0, rows, :], xs[r, part, 1, rows, :]
            imag = jnp.zeros_like(real) if r in (0, 8) else xs[r, part, 2, rows, :]
            blocks_.append(jnp.concatenate([real, imag], axis=1))
            blocks_.append(jnp.concatenate([imag, minus], axis=1))
        return jnp.concatenate(blocks_, axis=0)

    def product(r, pair):
        both = contract(table[r], operand(r, 0, pair))
        return both[:128] + both[128:] + contract(table[r, 0:128], operand(r, 1, pair))

    for r in range(8):
        for pair in range(inputs // 2):
            out = product(r, pair)
            if r == 0:
                out = out + product(8, pair)
            for h in range(2):
                send[pl.ds(r * inputs + 2 * pair + h, 128, stride=64), :] = out[:, h * LANES : (h + 1) * LANES]


def front(voltages, halo, taps, table):
    inputs, frames, nfft = voltages.shape
    vmem = pl.BlockSpec(memory_space=pltpu.VMEM)
    return pl.pallas_call(
        front_kernel,
        out_shape=jax.ShapeDtypeStruct((128 * 64, LANES), F32),
        in_specs=[pl.BlockSpec(memory_space=pl.ANY), vmem, vmem, vmem],
        out_specs=vmem,
        scratch_shapes=[
            pltpu.VMEM((inputs, nfft // LANES, frames + 8, LANES), F32),
            pltpu.VMEM((4, nfft // LANES, 8, LANES), F32),
            pltpu.VMEM((9, 2, 3, inputs * frames, LANES), BF16),
            pltpu.SemaphoreType.DMA((nfft // LANES,)),
        ],
        compiler_params=pltpu.CompilerParams(vmem_limit_bytes=48 << 20),
    )(voltages, halo, taps, table)


def correlate_kernel(recv, out):
    odd = lax.rem(lax.axis_index("tm"), 2)
    lane = lax.broadcasted_iota(jnp.int32, (256, LANES), 1)
    sign = jnp.where(lane < 64, 1.0, -1.0).astype(F32)
    for r in range(8):
        blocks, turns = [], []
        for t in range(4):
            block = recv[r, t]
            blocks.append(block)
            turns.append(pltpu.roll(block, 64, 1) * sign)
        plain = [split(b) for b in blocks]
        turned = [split(b) for b in turns]
        ph = jnp.concatenate([b[0] for b in plain], axis=1)
        plo = jnp.concatenate([b[1] for b in plain], axis=1)
        th = jnp.concatenate([b[0] for b in turned], axis=1)
        tlo = jnp.concatenate([b[1] for b in turned], axis=1)
        real = contract(ph, ph) + contract(ph, plo) + contract(plo, ph)
        imag = contract(th, ph) + contract(th, plo) + contract(tlo, ph)
        flip = 1.0 if r == 0 else jnp.where(odd == 1, -1.0, 1.0).astype(F32)
        chan = jnp.where(odd == 1, (8 - r) % 8, r)
        out[0, chan] = real
        out[1, chan] = imag * flip


def on_device(voltages, taps):
    frames = voltages.shape[1]
    table = jnp.asarray(tables(2048, 256))
    last = voltages[:, frames - 3 :, :]
    halo = lax.ppermute(last, "tm", [(0, 1), (1, 2), (2, 3)])
    send = front(voltages, halo, taps, table)
    got = lax.all_to_all(send.reshape(128, 8, 8, LANES), ("inp", "tm"), split_axis=0, concat_axis=0, tiled=True)
    got = got.reshape(32, 4, 8, 8, LANES).transpose(2, 1, 0, 3, 4).reshape(8, 4, 256, LANES)
    vmem = pl.BlockSpec(memory_space=pltpu.VMEM)
    return pl.pallas_call(
        correlate_kernel,
        out_shape=jax.ShapeDtypeStruct((2, 8, 256, 256), F32),
        in_specs=[vmem],
        out_specs=vmem,
        compiler_params=pltpu.CompilerParams(vmem_limit_bytes=48 << 20),
    )(got)


def solution(mesh):
    return jax.shard_map(
        on_device,
        mesh=mesh,
        in_specs=(P("inp", "tm", None), P()),
        out_specs=P(None, ("inp", "tm"), None, None),
        check_vma=False,
    )
```

time: 230 us -> 91.4 us (0.40)
  local copies, waits for them, and re-layouts: 59.1 us -> 3.63 us
  other arithmetic: 51.5 us -> 0 us
  matrix products: 48.5 us -> 0 us
  Pallas kernels: 0 us -> 14.2 us
  waiting for transfers between devices: 0.01 us -> 3.29 us
    dot_general x3 -> x0, matrix products: 48.5 us -> none  [the longest x1 32.5 us: on_device(): jnp.einsum('kn,ifn->kif', table, filtered, precision=lax.Precision.HIGHEST)]
    neg x2 -> x0, other arithmetic: 35.4 us -> none  [the longest x1 32.9 us: transform_table(): return jnp.concatenate([jnp.cos(angle), -jnp.sin(angle)], axis=0) * scale]
    unnamed x12 -> x4, local copies, waits for them, and re-layouts: 18.5 us -> 2.03 us
    reshape x2 -> x0, local copies, waits for them, and re-layouts: 15.2 us -> none  [on_device(): spectra = spectra.reshape(2, half, inputs_dev, frames_dev)]
    pallas_call x0 -> x2, Pallas kernels: none -> 14.2 us  [the longest x1 8.74 us: front(): pl.pallas_call(front_kernel, out_shape=jax.ShapeDtypeStruct((128 * 64, LA...]
    all_to_all x1 -> x0, other arithmetic: 13.8 us -> none  [on_device(): lax.all_to_all(spectra, ('inp', 'tm'), split_axis=1, concat_axis=2, tiled...]
    slice x5 -> x1, local copies, waits for them, and re-layouts: 10.8 us -> 1.1 us  [on_device(): last = voltages[:, frames - 3:, :]]
    squeeze x2 -> x0, local copies, waits for them, and re-layouts: 8.32 us -> none  [the longest x1 4.16 us: on_device(): spec_re = owned[0]]
  transfers between devices with their start and end apart: 1 -> 1, of which waited for: 0 -> 1; matrix products, arithmetic and copies ran while one was open for 14% -> 0% of each run, Pallas kernels for 0% -> 0%
where the time goes in v1:
time: 91.4 us; the launch traced here: 89.9 us
  blocking collectives  64.1 us (70%)
  Pallas kernels  14.2 us (16%)
  starting transfers between devices  4.59 us (5%)
  local copies, waits for them, and re-layouts  3.63 us (4%)
  waiting for transfers between devices  3.29 us (4%)
    all_to_all x1, blocking collectives, on_device(): lax.all_to_all(send.reshape(128, 8, 8, LANES), ('inp', 'tm'), split_axis=...  64.1 us
    pallas_call x1, Pallas kernels, front(): pl.pallas_call(front_kernel, out_shape=jax.ShapeDtypeStruct((128 * 64, LA...  8.74 us
    pallas_call x1, Pallas kernels, on_device(): pl.pallas_call(correlate_kernel, out_shape=jax.ShapeDtypeStruct((2, 8, 25...  5.48 us
    ppermute x1, starting transfers between devices, on_device(): halo = lax.ppermute(last, 'tm', [(0, 1), (1, 2), (2, 3)])  4.59 us
    ppermute x1, waiting for transfers between devices, on_device(): halo = lax.ppermute(last, 'tm', [(0, 1), (1, 2), (2, 3)])  3.29 us
    unnamed x4, local copies, waits for them, and re-layouts  2.03 us
  transfers between devices with their start and end apart: 1, of which 1 were waited for; matrix products, arithmetic and copies ran while one was open for 0% of the time, Pallas kernels for 0%

profile of v1, /device:TPU:1, one launch (start us, length us, event | category | flops | bytes accessed | tf_op | source)
XLA Modules:
  0.0 89.9 jit_solution(335841797047346482)
XLA Ops:
  0.0 1.1 %slice.3 = f32[8,3,2048]{2,1,0:T(4,128)S(1)} slice(f32[8,64,2048]{2,1,0:T(8,128)} %volt.1), slice={[0:8], [61:64], [0:2048]} | slice | bytes 393216 | tf_op jit(solution)/shard_map/slice | solution.py:184
  1.1 4.6 %collective-permute-start = (f32[8,3,2048]{2,1,0:T(4,128)S(1)}, f32[8,3,2048]{2,1,0:T(4,128)S(1)}, u32[]{:S(2)}, u32[]{:S(2)}) collective-permute-start(f32[8,3,2048]{2,1,0:T(4,128)S(1)} %slice.3), channel_id=1, source_target_pairs={{0,1},{1,2},{2,3},{4,5},{5,6},{6,7},{8,9},{9,10},{10,11},{12,13},{... | collective-permute-start | bytes 589832 | tf_op jit(solution)/shard_map/ppermute | solution.py:185
  5.7 3.3 %collective-permute-done.halo = f32[8,3,2048]{2,1,0:T(4,128)S(1)} collective-permute-done((f32[8,3,2048]{2,1,0:T(4,128)S(1)}, f32[8,3,2048]{2,1,0:T(4,128)S(1)}, u32[]{:S(2)}, u32[]{:S(2)}) %collective-permute-start) | collective-permute-done | bytes 196640 | tf_op jit(solution)/shard_map/ppermute | solution.py:185
  9.0 0.0 copy-start
  9.0 1.3 %copy-done = bf16[9,256,256]{2,1,0:T(8,128)(2,1)S(1)} copy-done((bf16[9,256,256]{2,1,0:T(8,128)(2,1)S(1)}, bf16[9,256,256]{2,1,0:T(8,128)(2,1)}, u32[]{:S(2)}) %copy-start) | copy-done | bytes 1179672
  10.3 0.0 copy-start.1
  10.3 0.8 copy-done.1
  11.0 8.7 %shard_map.37 = f32[8192,128]{1,0:T(8,128)S(1)} custom-call(f32[8,64,2048]{2,1,0:T(8,128)} %volt.1, f32[8,3,2048]{2,1,0:T(4,128)S(1)} %collective-permute-done.halo, f32[4,2048]{1,0:T(4,128)S(1)} %copy-done.1, bf16[9,256,256]{2,1,0:T(8,128)(2,1)S(1)} %copy-done), custom_call_target="tpu_custom_call" | custom-call | tf_op jit(solution)/shard_map/pallas_call | solution.py:142
  19.8 64.1 %all_to_all.5 = f32[128,8,8,128]{3,2,1,0:T(8,128)S(1)} all-to-all(f32[128,8,8,128]{3,2,1,0:T(8,128)S(1)} %bitcast.7), channel_id=1, replica_groups=mesh['inp'=32,'tm'=4] {'inp','tm'}, dimensions={0} | all-to-all | bytes 8388608 | tf_op jit(solution)/shard_map/all_to_all | solution.py:187
  83.9 0.5 copy.6
  84.4 5.5 %shard_map.38 = f32[2,8,256,256]{3,2,1,0:T(8,128)} custom-call(f32[8,4,256,128]{3,2,1,0:T(8,128)S(1)} %bitcast.8), custom_call_target="tpu_custom_call" | custom-call | tf_op jit(solution)/shard_map/pallas_call | solution.py:190
Async XLA Ops:
  1.1 7.9 %collective-permute-start = (f32[8,3,2048]{2,1,0:T(4,128)S(1)}, f32[8,3,2048]{2,1,0:T(4,128)S(1)}, u32[]{:S(2)}, u32[]{:S(2)}) collective-permute-start(f32[8,3,2048]{2,1,0:T(4,128)S(1)} %slice.3), channel_id=1, source_target_pairs={{0,1},{1,2},{2,3},{4,5},{5,6},{6,7},{8,9},{9,10},{10,11},{12,13},{... | collective-permute-start | bytes 589832 | tf_op jit(solution)/shard_map/ppermute | solution.py:185
  9.0 1.3 %copy-start = (bf16[9,256,256]{2,1,0:T(8,128)(2,1)S(1)}, bf16[9,256,256]{2,1,0:T(8,128)(2,1)}, u32[]{:S(2)}) copy-start(bf16[9,256,256]{2,1,0:T(8,128)(2,1)} %constant.2.clone.table) | copy-start | bytes 3538948
  10.3 0.8 copy-start.1

commit v2 on v1

v2 whole, which is shorter than its diff:
```python
import functools
import math

import jax
import jax.numpy as jnp
import numpy as np
from jax import lax
from jax.experimental import pallas as pl
from jax.experimental.pallas import tpu as pltpu
from jax.sharding import PartitionSpec as P

LANES = 128
F32 = jnp.float32
BF16 = jnp.bfloat16


def tables(nfft, spectra):
    dests = 128
    n2 = np.arange(LANES)
    scale = 1.0 / math.sqrt(nfft) / math.sqrt(spectra)
    out = np.zeros((9, dests, 2 * LANES), np.float64)
    for r in range(9):
        for m in range(dests):
            if (r == 0 and m % 2 == 1) or (r == 8 and m % 2 == 0):
                continue
            q = m // 2 if (m % 2 == 0 or r == 8) else 127 - m // 2
            angle = 2.0 * np.pi * ((n2 * (16 * q + r)) % nfft) / nfft
            out[r, m, :LANES] = np.cos(angle) * scale
            out[r, m, LANES:] = np.sin(angle) * scale
    out = out.astype(np.float32)
    high = out.astype(jnp.bfloat16)
    low = (out - high.astype(np.float32)).astype(jnp.bfloat16)
    return np.concatenate([high, low], axis=1)


def split(value):
    high = value.astype(BF16)
    return high, (value - high.astype(F32)).astype(BF16)


def sixteen(x):
    c1, c2, c3 = (math.cos(k * math.pi / 8) for k in (1, 2, 3))
    a = [x[n] + x[n + 8] for n in range(8)]
    b = [x[n] - x[n + 8] for n in range(8)]
    c = [a[n] + a[n + 4] for n in range(4)]
    d = [a[n] - a[n + 4] for n in range(4)]
    c02, c13 = c[0] + c[2], c[1] + c[3]
    y = {0: (c02 + c13, None), 8: (c02 - c13, None), 4: (c[0] - c[2], c[3] - c[1])}
    dm, dp = (d[1] - d[3]) * c2, (d[1] + d[3]) * c2
    y[2] = (d[0] + dm, -(d[2] + dp))
    y[6] = (d[0] - dm, d[2] - dp)
    e = [None] + [b[n] - b[8 - n] for n in (1, 2, 3)]
    g = [None] + [b[n] + b[8 - n] for n in (1, 2, 3)]
    e2, g2 = e[2] * c2, g[2] * c2
    p, q = b[0] + e2, b[0] - e2
    s, t = e[1] * c1 + e[3] * c3, e[1] * c3 - e[3] * c1
    v, w = b[4] + g2, g2 - b[4]
    h, k = g[1] * c3 + g[3] * c1, g[1] * c1 - g[3] * c3
    y[1] = (p + s, -(v + h))
    y[7] = (p - s, v - h)
    y[3] = (q + t, -(k + w))
    y[5] = (q - t, w - k)
    return y


def contract(a, b):
    return lax.dot_general(a, b, (((1,), (1,)), ((), ())), preferred_element_type=F32)


MESH = pl.DeviceIdType.MESH
GROUPS = ((0, 1), (1, 2), (3, 2), (5, 2), (7, 1))
DEVICES = 128


def place():
    inp, tm = lax.axis_index("inp"), lax.axis_index("tm")
    return inp, tm, (lax.rem(inp // 4, 4), inp // 16 * 2 + tm // 2, lax.rem(inp, 4), lax.rem(tm, 2))


def partner(here, step):
    x, y, z, core = here
    k = lax.rem(step * 37, DEVICES)
    core = lax.rem(core + k, 2)
    x = lax.rem(x + k // 2, 4)
    y = lax.rem(y + k // 8, 4)
    z = lax.rem(z + k // 32, 4)
    return y // 2 * 16 + x * 4 + z, lax.rem(y, 2) * 2 + core


def kernel(volt, taps, table, out, ext, tapb, xs, send, recv, load_sem, halo_sem, send_sem, recv_sem):
    inputs, frames = volt.shape[0], volt.shape[1]
    blocks = volt.shape[2] // LANES
    inp, tm, here = place()
    me = inp * 4 + tm

    barrier = pltpu.get_barrier_semaphore()
    loads = []
    for l in range(blocks):
        lanes = pl.ds(l * LANES, LANES)
        loads.append(pltpu.make_async_copy(volt.at[:, :, lanes], ext.at[:, l, pl.ds(8, frames), :], load_sem.at[l]))
        loads[-1].start()

    @pl.loop(1, DEVICES)
    def _(k):
        other = lax.rem(me + k, DEVICES)
        pl.semaphore_signal(barrier, inc=1, device_id=(other // 4, lax.rem(other, 4)), device_id_type=MESH)

    for k in range(4):
        for l in range(blocks):
            tapb[k, l] = jnp.broadcast_to(taps[k : k + 1, l * LANES : (l + 1) * LANES], (8, LANES))
    for load in loads:
        load.wait()
    pl.semaphore_wait(barrier, DEVICES - 1)

    halo = pltpu.make_async_remote_copy(
        src_ref=ext.at[:, :, pl.ds(5 + frames, 3), :],
        dst_ref=ext.at[:, :, pl.ds(5, 3), :],
        send_sem=halo_sem.at[0],
        recv_sem=halo_sem.at[1],
        device_id=(inp, lax.rem(tm + 1, 4)),
        device_id_type=MESH,
    )

    @pl.when(tm < 3)
    def _():
        halo.start()

    step = 16

    def filtered(i, f):
        parts = []
        for l in range(blocks):
            halves = []
            for j in range(step // 8):
                row = 5 + f * step + j * 8
                acc = tapb[0, l] * ext[i, l, pl.ds(row, 8), :]
                for k in range(1, 4):
                    acc = acc + tapb[k, l] * ext[i, l, pl.ds(row + k, 8), :]
                halves.append(acc)
            parts.append(jnp.concatenate(halves, axis=0))
        y = sixteen(parts)
        rows = pl.ds(pl.multiple_of(i * frames, frames) + f * step, step)
        for r in range(9):
            real, imag = y[r]
            high, low = split(real)
            xs[r, 0, 0, rows, :] = high
            xs[r, 1, 0, rows, :] = low
            xs[r, 0, 1, rows, :] = -high
            xs[r, 1, 1, rows, :] = -low
            if imag is not None:
                high, low = split(imag)
                xs[r, 0, 2, rows, :] = high
                xs[r, 1, 2, rows, :] = low

    @pl.loop(0, inputs)
    def _(i):
        for f in range(1, frames // step):
            filtered(i, f)

    @pl.when(tm > 0)
    def _():
        halo.wait_recv()

    @pl.when(tm == 0)
    def _():
        @pl.loop(0, inputs)
        def _(i):
            for l in range(blocks):
                ext[i, l, 5:8, :] = jnp.zeros((3, LANES), F32)

    @pl.loop(0, inputs)
    def _(i):
        filtered(i, 0)

    @pl.when(tm < 3)
    def _():
        halo.wait_send()

    def operand(r, part, pair):
        rows_ = []
        for i in (2 * pair, 2 * pair + 1):
            rows = pl.ds(i * frames, frames)
            real, minus = xs[r, part, 0, rows, :], xs[r, part, 1, rows, :]
            imag = jnp.zeros_like(real) if r in (0, 8) else xs[r, part, 2, rows, :]
            rows_.append(jnp.concatenate([real, imag], axis=1))
            rows_.append(jnp.concatenate([imag, minus], axis=1))
        return jnp.concatenate(rows_, axis=0)

    def product(r, pair):
        both = contract(table[r], operand(r, 0, pair))
        return both[:128] + both[128:] + contract(table[r, 0:128], operand(r, 1, pair))

    flat = send.reshape(DEVICES * 64, LANES)
    for g, (first, count) in enumerate(GROUPS):
        for r in range(first, first + count):
            for pair in range(inputs // 2):
                value = product(r, pair)
                if r == 0:
                    value = value + product(8, pair)
                for h in range(2):
                    flat[pl.ds(r * inputs + 2 * pair + h, DEVICES, stride=64), :] = value[:, h * LANES : (h + 1) * LANES]
        slots = pl.ds(first, count)
        target = recv.at[slots, tm, pl.ds(pl.multiple_of(inp * 8, 8), 8), :]
        pltpu.make_async_copy(send.at[me, slots], target, recv_sem.at[g]).start()

        @pl.loop(1, DEVICES)
        def _(k):
            to_inp, to_tm = partner(here, k)
            pltpu.make_async_remote_copy(
                src_ref=send.at[to_inp * 4 + to_tm, slots],
                dst_ref=target,
                send_sem=send_sem,
                recv_sem=recv_sem.at[g],
                device_id=(to_inp, to_tm),
                device_id_type=MESH,
            ).start()

    lane = lax.broadcasted_iota(jnp.int32, (256, LANES), 1)
    sign = jnp.where(lane < 64, 1.0, -1.0).astype(F32)
    odd = lax.rem(tm, 2)
    for g, (first, count) in enumerate(GROUPS):
        slots = recv.at[pl.ds(first, count)]
        pltpu.make_async_copy(slots, slots, recv_sem.at[g]).wait()
        for r in range(first, first + count):
            blocks_, turns = [], []
            for t in range(4):
                block = recv[r, t]
                blocks_.append(split(block))
                turns.append(split(pltpu.roll(block, 64, 1) * sign))
            ph, plo, th, tlo = (jnp.concatenate([b[part] for b in of], axis=1) for of in (blocks_, turns) for part in (0, 1))
            real = contract(ph, ph) + contract(ph, plo) + contract(plo, ph)
            imag = contract(th, ph) + contract(th, plo) + contract(tlo, ph)
            flip = 1.0 if r == 0 else jnp.where(odd == 1, -1.0, 1.0).astype(F32)
            chan = jnp.where(odd == 1, (8 - r) % 8, r)
            out[0, chan] = real
            out[1, chan] = imag * flip
    sent = send.at[pl.ds(0, DEVICES - 1)]
    pltpu.make_async_copy(sent, sent, send_sem).wait()


def on_device(voltages, taps):
    inputs, frames, nfft = voltages.shape
    table = jnp.asarray(tables(nfft, 4 * frames))
    vmem = pl.BlockSpec(memory_space=pltpu.VMEM)
    return pl.pallas_call(
        kernel,
        out_shape=jax.ShapeDtypeStruct((2, 8, 256, 256), F32),
        in_specs=[pl.BlockSpec(memory_space=pl.ANY), vmem, vmem],
        out_specs=vmem,
        scratch_shapes=[
            pltpu.VMEM((inputs, nfft // LANES, frames + 8, LANES), F32),
            pltpu.VMEM((4, nfft // LANES, 8, LANES), F32),
            pltpu.VMEM((9, 2, 3, inputs * frames, LANES), BF16),
            pltpu.VMEM((DEVICES, 8, inputs, LANES), F32),
            pltpu.VMEM((8, 4, 256, LANES), F32),
            pltpu.SemaphoreType.DMA((nfft // LANES,)),
            pltpu.SemaphoreType.DMA((2,)),
            pltpu.SemaphoreType.DMA,
            pltpu.SemaphoreType.DMA((len(GROUPS),)),
        ],
        compiler_params=pltpu.CompilerParams(collective_id=0, has_side_effects=True, vmem_limit_bytes=40 << 20),
    )(voltages, taps, table)


def solution(mesh):
    return jax.shard_map(
        on_device,
        mesh=mesh,
        in_specs=(P("inp", "tm", None), P()),
        out_specs=P(None, ("inp", "tm"), None, None),
        check_vma=False,
    )
```

time: 91.4 us -> 72.7 us (0.80); the launches traced: 89.9 us -> 72.4 us
  blocking collectives: 64.1 us -> 0 us
  Pallas kernels: 14.2 us -> 66.2 us
  starting transfers between devices: 4.59 us -> 0 us
  waiting for transfers between devices: 3.29 us -> 0 us
  local copies, waits for them, and re-layouts: 3.63 us -> 6.23 us
    all_to_all x1 -> x0, blocking collectives: 64.1 us -> none  [on_device(): lax.all_to_all(send.reshape(128, 8, 8, LANES), ('inp', 'tm'), split_axis=...]
    pallas_call x2 -> x1, Pallas kernels: 14.2 us -> 66.2 us  [on_device(): pl.pallas_call(kernel, out_shape=jax.ShapeDtypeStruct((2, 8, 256, 256), F...]
    ppermute x1 -> x0, starting transfers between devices: 4.59 us -> none  [on_device(): halo = lax.ppermute(last, 'tm', [(0, 1), (1, 2), (2, 3)])]
    unnamed x4 -> x7, local copies, waits for them, and re-layouts: 2.03 us -> 6.23 us
    ppermute x1 -> x0, waiting for transfers between devices: 3.29 us -> none  [on_device(): halo = lax.ppermute(last, 'tm', [(0, 1), (1, 2), (2, 3)])]
    slice x1 -> x0, local copies, waits for them, and re-layouts: 1.1 us -> none  [on_device(): last = voltages[:, frames - 3:, :]]
  transfers between devices with their start and end apart: 1 -> 0, of which waited for: 1 -> 0; matrix products, arithmetic and copies ran while one was open for 0% -> 0% of each run, Pallas kernels for 0% -> 0%
where the time goes in v2:
time: 72.7 us; the launch traced here: 72.4 us
  Pallas kernels  66.2 us (91%)
  local copies, waits for them, and re-layouts  6.23 us (9%)
    pallas_call x1, Pallas kernels, on_device(): pl.pallas_call(kernel, out_shape=jax.ShapeDtypeStruct((2, 8, 256, 256), F...  66.2 us
    unnamed x7, local copies, waits for them, and re-layouts  6.23 us

profile of v2, /device:TPU:1, one launch (start us, length us, event | category | flops | bytes accessed | tf_op | source)
XLA Modules:
  0.0 72.4 jit_solution(11015709536126369658)
XLA Ops:
  0.0 0.0 copy-start
  0.0 2.2 %copy-done = f32[8,64,2048]{2,1,0:T(8,128)S(1)} copy-done((f32[8,64,2048]{2,1,0:T(8,128)S(1)}, f32[8,64,2048]{2,1,0:T(8,128)}, u32[]{:S(2)}) %copy-start) | copy-done | bytes 4194328
  2.2 0.0 copy-start.1
  2.2 1.3 %copy-done.1 = bf16[9,256,256]{2,1,0:T(8,128)(2,1)S(1)} copy-done((bf16[9,256,256]{2,1,0:T(8,128)(2,1)S(1)}, bf16[9,256,256]{2,1,0:T(8,128)(2,1)}, u32[]{:S(2)}) %copy-start.1) | copy-done | bytes 1179672
  3.5 0.0 copy-start.2
  3.5 0.8 %copy-done.2 = f32[4,2048]{1,0:T(4,128)S(1)} copy-done((f32[4,2048]{1,0:T(4,128)S(1)}, f32[4,2048]{1,0:T(4,128)}, u32[]{:S(2)}) %copy-start.2) | copy-done | bytes 32792
  4.2 66.2 %shard_map.37 = f32[2,8,256,256]{3,2,1,0:T(8,128)S(1)} custom-call(f32[8,64,2048]{2,1,0:T(8,128)S(1)} %copy-done, f32[4,2048]{1,0:T(4,128)S(1)} %copy-done.2, bf16[9,256,256]{2,1,0:T(8,128)(2,1)S(1)} %copy-done.1), custom_call_target="tpu_custom_call" | custom-call | tf_op jit(solution)/shard_map/pallas_call | solution.py:245
  70.4 2.0 %copy.5 = f32[2,8,256,256]{3,2,1,0:T(8,128)} copy(f32[2,8,256,256]{3,2,1,0:T(8,128)S(1)} %shard_map.37) | data formatting | bytes 8388608
Async XLA Ops:
  0.0 2.2 %copy-start = (f32[8,64,2048]{2,1,0:T(8,128)S(1)}, f32[8,64,2048]{2,1,0:T(8,128)}, u32[]{:S(2)}) copy-start(f32[8,64,2048]{2,1,0:T(8,128)} %volt.1) | copy-start | bytes 12582916
  2.2 1.3 %copy-start.1 = (bf16[9,256,256]{2,1,0:T(8,128)(2,1)S(1)}, bf16[9,256,256]{2,1,0:T(8,128)(2,1)}, u32[]{:S(2)}) copy-start(bf16[9,256,256]{2,1,0:T(8,128)(2,1)} %constant.2.clone.table) | copy-start | bytes 3538948
  3.5 0.8 %copy-start.2 = (f32[4,2048]{1,0:T(4,128)S(1)}, f32[4,2048]{1,0:T(4,128)}, u32[]{:S(2)}) copy-start(f32[4,2048]{1,0:T(4,128)} %taps.1) | copy-start | bytes 98308

commit v3 on v2

--- a/solution.py
+++ b/solution.py
@@ -68,7 +68,7 @@
 
 
 MESH = pl.DeviceIdType.MESH
-GROUPS = ((0, 1), (1, 2), (3, 2), (5, 2), (7, 1))
+GROUPS = ((0, 2), (2, 2), (4, 2), (6, 1), (7, 1))
 DEVICES = 128
 
 
@@ -87,43 +87,71 @@
     return y // 2 * 16 + x * 4 + z, lax.rem(y, 2) * 2 + core
 
 
-def kernel(volt, taps, table, out, ext, tapb, xs, send, recv, load_sem, halo_sem, send_sem, recv_sem):
+def kernel(volt, taps_hbm, table_hbm, out, taps, table, ext, tapb, xs, send, recv, load_sem, halo_send, halo_recv, line_sem, send_sem, recv_sem):
     inputs, frames = volt.shape[0], volt.shape[1]
     blocks = volt.shape[2] // LANES
     inp, tm, here = place()
     me = inp * 4 + tm
 
+    high, x, z = inp // 16 * 16, lax.rem(inp // 4, 4) * 4, lax.rem(inp, 4)
+    line_z = [(high + x + lax.rem(z + k, 4), tm) for k in (1, 2, 3)]
+    line_x = [(high + lax.rem(x + 4 * k, 16) + z, tm) for k in (1, 2, 3)]
+    line_y = [(lax.rem(inp + 16, 32), tm)]
+    line_t = [(inp, lax.rem(tm + k, 4)) for k in (1, 2, 3)]
+    lines = (line_z, line_x, line_y)
+
+    def greet(line, sem):
+        for device in line:
+            pl.semaphore_signal(sem, inc=1, device_id=device, device_id_type=MESH)
+
     barrier = pltpu.get_barrier_semaphore()
-    loads = []
+    for line in (line_t, *lines):
+        greet(line, barrier)
+
+    loads = [
+        pltpu.make_async_copy(taps_hbm, taps, load_sem.at[blocks]),
+        pltpu.make_async_copy(table_hbm, table, load_sem.at[blocks + 1]),
+    ]
+    loads[0].start()
     for l in range(blocks):
         lanes = pl.ds(l * LANES, LANES)
         loads.append(pltpu.make_async_copy(volt.at[:, :, lanes], ext.at[:, l, pl.ds(8, frames), :], load_sem.at[l]))
         loads[-1].start()
-
-    @pl.loop(1, DEVICES)
-    def _(k):
-        other = lax.rem(me + k, DEVICES)
-        pl.semaphore_signal(barrier, inc=1, device_id=(other // 4, lax.rem(other, 4)), device_id_type=MESH)
-
+    loads[1].start()
+
+    pl.semaphore_wait(barrier, 10)
+    halos = [
+        pltpu.make_async_remote_copy(
+            src_ref=volt.at[:, pl.ds(frames - 3, 3), pl.ds(l * LANES, LANES)],
+            dst_ref=ext.at[:, l, pl.ds(5, 3), :],
+            send_sem=halo_send.at[l],
+            recv_sem=halo_recv.at[l],
+            device_id=(inp, lax.rem(tm + 1, 4)),
+            device_id_type=MESH,
+        )
+        for l in range(blocks)
+    ]
+
+    @pl.when(tm < 3)
+    def _():
+        for halo in halos:
+            halo.start()
+
+    greet(line_z, line_sem.at[0])
+
+    @pl.when(tm == 0)
+    def _():
+        @pl.loop(0, inputs)
+        def _(i):
+            for l in range(blocks):
+                ext[i, l, 5:8, :] = jnp.zeros((3, LANES), F32)
+
+    loads[0].wait()
     for k in range(4):
         for l in range(blocks):
             tapb[k, l] = jnp.broadcast_to(taps[k : k + 1, l * LANES : (l + 1) * LANES], (8, LANES))
-    for load in loads:
+    for load in loads[2:]:
         load.wait()
-    pl.semaphore_wait(barrier, DEVICES - 1)
-
-    halo = pltpu.make_async_remote_copy(
-        src_ref=ext.at[:, :, pl.ds(5 + frames, 3), :],
-        dst_ref=ext.at[:, :, pl.ds(5, 3), :],
-        send_sem=halo_sem.at[0],
-        recv_sem=halo_sem.at[1],
-        device_id=(inp, lax.rem(tm + 1, 4)),
-        device_id_type=MESH,
-    )
-
-    @pl.when(tm < 3)
-    def _():
-        halo.start()
 
     step = 16
 
@@ -152,29 +180,31 @@
                 xs[r, 0, 2, rows, :] = high
                 xs[r, 1, 2, rows, :] = low
 
-    @pl.loop(0, inputs)
-    def _(i):
-        for f in range(1, frames // step):
-            filtered(i, f)
+    def later(first, last):
+        @pl.loop(first, last)
+        def _(i):
+            for f in range(1, frames // step):
+                filtered(i, f)
+
+    later(0, 2)
+    pl.semaphore_wait(line_sem.at[0], 3)
+    greet(line_x, line_sem.at[1])
+    later(2, 5)
+    pl.semaphore_wait(line_sem.at[1], 3)
+    greet(line_y, line_sem.at[2])
+    later(5, inputs)
 
     @pl.when(tm > 0)
     def _():
-        halo.wait_recv()
-
-    @pl.when(tm == 0)
-    def _():
-        @pl.loop(0, inputs)
-        def _(i):
-            for l in range(blocks):
-                ext[i, l, 5:8, :] = jnp.zeros((3, LANES), F32)
+        for halo in halos:
+            halo.wait_recv()
 
     @pl.loop(0, inputs)
     def _(i):
         filtered(i, 0)
 
-    @pl.when(tm < 3)
-    def _():
-        halo.wait_send()
+    loads[1].wait()
+    pl.semaphore_wait(line_sem.at[2], 1)
 
     def operand(r, part, pair):
         rows_ = []
@@ -234,6 +264,12 @@
             chan = jnp.where(odd == 1, (8 - r) % 8, r)
             out[0, chan] = real
             out[1, chan] = imag * flip
+
+    @pl.when(tm < 3)
+    def _():
+        for halo in halos:
+            halo.wait_send()
+
     sent = send.at[pl.ds(0, DEVICES - 1)]
     pltpu.make_async_copy(sent, sent, send_sem).wait()
 
@@ -242,24 +278,29 @@
     inputs, frames, nfft = voltages.shape
     table = jnp.asarray(tables(nfft, 4 * frames))
     vmem = pl.BlockSpec(memory_space=pltpu.VMEM)
+    hbm = pl.BlockSpec(memory_space=pltpu.HBM)
     return pl.pallas_call(
         kernel,
         out_shape=jax.ShapeDtypeStruct((2, 8, 256, 256), F32),
-        in_specs=[pl.BlockSpec(memory_space=pl.ANY), vmem, vmem],
+        in_specs=[hbm, hbm, hbm],
         out_specs=vmem,
         scratch_shapes=[
+            pltpu.VMEM(taps.shape, F32),
+            pltpu.VMEM(table.shape, BF16),
             pltpu.VMEM((inputs, nfft // LANES, frames + 8, LANES), F32),
             pltpu.VMEM((4, nfft // LANES, 8, LANES), F32),
             pltpu.VMEM((9, 2, 3, inputs * frames, LANES), BF16),
             pltpu.VMEM((DEVICES, 8, inputs, LANES), F32),
             pltpu.VMEM((8, 4, 256, LANES), F32),
+            pltpu.SemaphoreType.DMA((nfft // LANES + 2,)),
             pltpu.SemaphoreType.DMA((nfft // LANES,)),
-            pltpu.SemaphoreType.DMA((2,)),
+            pltpu.SemaphoreType.DMA((nfft // LANES,)),
+            pltpu.SemaphoreType.REGULAR((3,)),
             pltpu.SemaphoreType.DMA,
             pltpu.SemaphoreType.DMA((len(GROUPS),)),
         ],
         compiler_params=pltpu.CompilerParams(collective_id=0, has_side_effects=True, vmem_limit_bytes=40 << 20),
-    )(voltages, taps, table)
+    )(*(pltpu.with_memory_space_constraint(v, pltpu.HBM) for v in (voltages, taps, table)))
 
 
 def solution(mesh):

time: 72.7 us -> 65.5 us (0.901)
  local copies, waits for them, and re-layouts: 6.23 us -> 2.02 us
  Pallas kernels: 66.2 us -> 63.4 us
    unnamed x7 -> x1, local copies, waits for them, and re-layouts: 6.23 us -> 2.02 us
    pallas_call x1, Pallas kernels: 66.2 us -> 63.4 us  [on_device(): pl.pallas_call(kernel, out_shape=jax.ShapeDtypeStruct((2, 8, 256, 256), F...]
where the time goes in v3:
time: 65.5 us; the launch traced here: 65.4 us
  Pallas kernels  63.4 us (97%)
  local copies, waits for them, and re-layouts  2.02 us (3%)
    pallas_call x1, Pallas kernels, on_device(): pl.pallas_call(kernel, out_shape=jax.ShapeDtypeStruct((2, 8, 256, 256), F...  63.4 us
    unnamed x1, local copies, waits for them, and re-layouts  2.02 us

profile of v3, /device:TPU:1, one launch (start us, length us, event | category | flops | bytes accessed | tf_op | source)
XLA Modules:
  0.0 65.4 jit_solution(8582578239600265107)
XLA Ops:
  0.0 63.4 %shard_map.37 = f32[2,8,256,256]{3,2,1,0:T(8,128)S(1)} custom-call(f32[8,64,2048]{2,1,0:T(8,128)} %volt.1, f32[4,2048]{1,0:T(4,128)} %taps_hbm.1, bf16[9,256,256]{2,1,0:T(8,128)(2,1)} %constant.2.clone.table_hbm), custom_call_target="tpu_custom_call" | custom-call | tf_op jit(solution)/shard_map/pallas_call | solution.py:282
  63.4 2.0 %copy.5 = f32[2,8,256,256]{3,2,1,0:T(8,128)} copy(f32[2,8,256,256]{3,2,1,0:T(8,128)S(1)} %shard_map.37) | data formatting | bytes 8388608

commit v4 on v3

--- a/solution.py
+++ b/solution.py
@@ -77,36 +77,59 @@
     return inp, tm, (lax.rem(inp // 4, 4), inp // 16 * 2 + tm // 2, lax.rem(inp, 4), lax.rem(tm, 2))
 
 
-def partner(here, step):
-    x, y, z, core = here
-    k = lax.rem(step * 37, DEVICES)
-    core = lax.rem(core + k, 2)
-    x = lax.rem(x + k // 2, 4)
-    y = lax.rem(y + k // 8, 4)
-    z = lax.rem(z + k // 32, 4)
-    return y // 2 * 16 + x * 4 + z, lax.rem(y, 2) * 2 + core
-
-
-def kernel(volt, taps_hbm, table_hbm, out, taps, table, ext, tapb, xs, send, recv, load_sem, halo_send, halo_recv, line_sem, send_sem, recv_sem):
+def offsets():
+    shuffled = np.random.RandomState(1).permutation(np.arange(1, DEVICES))
+    steps = [(int(k) // 2 % 4, int(k) // 8 % 4, int(k) // 32, int(k) % 2) for k in shuffled]
+    return sorted(steps, key=lambda step: -sum(min(d, 4 - d) for d in step[:3]))
+
+
+def visibility(blocks, r, tm):
+    odd = lax.rem(tm, 2)
+    lane = lax.broadcasted_iota(jnp.int32, (256, LANES), 1)
+    sign = jnp.where(lane < 64, 1.0, -1.0).astype(F32)
+    plain = [split(b) for b in blocks]
+    turned = [split(pltpu.roll(b, 64, 1) * sign) for b in blocks]
+    ph, plo, th, tlo = (jnp.concatenate([b[part] for b in of], axis=1) for of in (plain, turned) for part in (0, 1))
+    real = contract(ph, ph) + contract(ph, plo) + contract(plo, ph)
+    imag = contract(th, ph) + contract(th, plo) + contract(tlo, ph)
+    flip = 1.0 if r == 0 else jnp.where(odd == 1, -1.0, 1.0).astype(F32)
+    return jnp.where(odd == 1, (8 - r) % 8, r), real, imag * flip
+
+
+def tail_kernel(begun, last, out, stage, sem):
+    tm = lax.axis_index("tm")
+    final = jnp.where(lax.rem(tm, 2) == 1, 1, 7)
+    writes = []
+    for k in range(1, 8):
+        chan = lax.rem(final + k, 8)
+        writes.append(pltpu.make_async_copy(begun.at[:, chan], out.at[:, chan], sem.at[k]))
+        writes[-1].start()
+    chan, real, imag = visibility([last[0, t] for t in range(4)], 7, tm)
+    stage[0] = real
+    stage[1] = imag
+    writes.append(pltpu.make_async_copy(stage, out.at[:, chan], sem.at[0]))
+    writes[-1].start()
+    for write in writes:
+        write.wait()
+
+
+def kernel(volt, taps_hbm, table_hbm, out, last, taps, table, ext, tapb, xs, send, recv, load_sem, halo_send, halo_recv, column_sem, send_sem, recv_sem):
     inputs, frames = volt.shape[0], volt.shape[1]
     blocks = volt.shape[2] // LANES
     inp, tm, here = place()
     me = inp * 4 + tm
 
-    high, x, z = inp // 16 * 16, lax.rem(inp // 4, 4) * 4, lax.rem(inp, 4)
-    line_z = [(high + x + lax.rem(z + k, 4), tm) for k in (1, 2, 3)]
-    line_x = [(high + lax.rem(x + 4 * k, 16) + z, tm) for k in (1, 2, 3)]
-    line_y = [(lax.rem(inp + 16, 32), tm)]
-    line_t = [(inp, lax.rem(tm + k, 4)) for k in (1, 2, 3)]
-    lines = (line_z, line_x, line_y)
+    high, low = inp // 16 * 16, lax.rem(inp, 16)
+    plane = [(high + lax.rem(low + k, 16), tm) for k in range(1, 16)]
+    column = [(inp, lax.rem(tm + k, 4)) for k in (1, 2, 3)] + [(lax.rem(inp + 16, 32), lax.rem(tm + k, 4)) for k in range(4)]
 
     def greet(line, sem):
         for device in line:
             pl.semaphore_signal(sem, inc=1, device_id=device, device_id_type=MESH)
 
     barrier = pltpu.get_barrier_semaphore()
-    for line in (line_t, *lines):
-        greet(line, barrier)
+    greet(column, barrier)
+    greet(plane, barrier)
 
     loads = [
         pltpu.make_async_copy(taps_hbm, taps, load_sem.at[blocks]),
@@ -119,7 +142,8 @@
         loads[-1].start()
     loads[1].start()
 
-    pl.semaphore_wait(barrier, 10)
+    pl.semaphore_wait(barrier, 22)
+    greet(column, column_sem)
     halos = [
         pltpu.make_async_remote_copy(
             src_ref=volt.at[:, pl.ds(frames - 3, 3), pl.ds(l * LANES, LANES)],
@@ -136,8 +160,6 @@
     def _():
         for halo in halos:
             halo.start()
-
-    greet(line_z, line_sem.at[0])
 
     @pl.when(tm == 0)
     def _():
@@ -186,13 +208,7 @@
             for f in range(1, frames // step):
                 filtered(i, f)
 
-    later(0, 2)
-    pl.semaphore_wait(line_sem.at[0], 3)
-    greet(line_x, line_sem.at[1])
-    later(2, 5)
-    pl.semaphore_wait(line_sem.at[1], 3)
-    greet(line_y, line_sem.at[2])
-    later(5, inputs)
+    later(0, inputs)
 
     @pl.when(tm > 0)
     def _():
@@ -204,7 +220,7 @@
         filtered(i, 0)
 
     loads[1].wait()
-    pl.semaphore_wait(line_sem.at[2], 1)
+    pl.semaphore_wait(column_sem, 7)
 
     def operand(r, part, pair):
         rows_ = []
@@ -221,50 +237,57 @@
         return both[:128] + both[128:] + contract(table[r, 0:128], operand(r, 1, pair))
 
     flat = send.reshape(DEVICES * 64, LANES)
+
+    def fill(r):
+        for pair in range(inputs // 2):
+            value = product(r, pair)
+            if r == 0:
+                value = value + product(8, pair)
+            for h in range(2):
+                flat[pl.ds(r * inputs + 2 * pair + h, DEVICES, stride=64), :] = value[:, h * LANES : (h + 1) * LANES]
+
+    rows = pl.ds(pl.multiple_of(inp * 8, 8), 8)
+
+    def landing(first, count):
+        return last.at[pl.ds(0, 1), tm, rows, :] if first == 7 else recv.at[pl.ds(first, count), tm, rows, :]
+
+    def ship(g, to_inp, to_tm):
+        first, count = GROUPS[g]
+        pltpu.make_async_remote_copy(
+            src_ref=send.at[to_inp * 4 + to_tm, pl.ds(first, count)],
+            dst_ref=landing(first, count),
+            send_sem=send_sem,
+            recv_sem=recv_sem.at[g],
+            device_id=(to_inp, to_tm),
+            device_id_type=MESH,
+        ).start()
+
+    x, y, z, core = here
+    x_at = [lax.rem(x + j, 4) * 4 for j in range(4)]
+    y_at = [lax.rem(y + j, 4) for j in range(4)]
+    y_at = [(at // 2 * 16, lax.rem(at, 2) * 2) for at in y_at]
+    z_at = [lax.rem(z + j, 4) for j in range(4)]
+    core_at = [core, 1 - core]
+
+    def exchange(g):
+        first, count = GROUPS[g]
+        pltpu.make_async_copy(send.at[me, pl.ds(first, count)], landing(first, count), recv_sem.at[g]).start()
+        for dx, dy, dz, dc in offsets():
+            ship(g, y_at[dy][0] + x_at[dx] + z_at[dz], y_at[dy][1] + core_at[dc])
+
     for g, (first, count) in enumerate(GROUPS):
         for r in range(first, first + count):
-            for pair in range(inputs // 2):
-                value = product(r, pair)
-                if r == 0:
-                    value = value + product(8, pair)
-                for h in range(2):
-                    flat[pl.ds(r * inputs + 2 * pair + h, DEVICES, stride=64), :] = value[:, h * LANES : (h + 1) * LANES]
-        slots = pl.ds(first, count)
-        target = recv.at[slots, tm, pl.ds(pl.multiple_of(inp * 8, 8), 8), :]
-        pltpu.make_async_copy(send.at[me, slots], target, recv_sem.at[g]).start()
-
-        @pl.loop(1, DEVICES)
-        def _(k):
-            to_inp, to_tm = partner(here, k)
-            pltpu.make_async_remote_copy(
-                src_ref=send.at[to_inp * 4 + to_tm, slots],
-                dst_ref=target,
-                send_sem=send_sem,
-                recv_sem=recv_sem.at[g],
-                device_id=(to_inp, to_tm),
-                device_id_type=MESH,
-            ).start()
-
-    lane = lax.broadcasted_iota(jnp.int32, (256, LANES), 1)
-    sign = jnp.where(lane < 64, 1.0, -1.0).astype(F32)
-    odd = lax.rem(tm, 2)
-    for g, (first, count) in enumerate(GROUPS):
+            fill(r)
+        exchange(g)
+
+    for g, (first, count) in enumerate(GROUPS[:-1]):
         slots = recv.at[pl.ds(first, count)]
         pltpu.make_async_copy(slots, slots, recv_sem.at[g]).wait()
         for r in range(first, first + count):
-            blocks_, turns = [], []
-            for t in range(4):
-                block = recv[r, t]
-                blocks_.append(split(block))
-                turns.append(split(pltpu.roll(block, 64, 1) * sign))
-            ph, plo, th, tlo = (jnp.concatenate([b[part] for b in of], axis=1) for of in (blocks_, turns) for part in (0, 1))
-            real = contract(ph, ph) + contract(ph, plo) + contract(plo, ph)
-            imag = contract(th, ph) + contract(th, plo) + contract(tlo, ph)
-            flip = 1.0 if r == 0 else jnp.where(odd == 1, -1.0, 1.0).astype(F32)
-            chan = jnp.where(odd == 1, (8 - r) % 8, r)
+            chan, real, imag = visibility([recv[r, t] for t in range(4)], r, tm)
             out[0, chan] = real
-            out[1, chan] = imag * flip
-
+            out[1, chan] = imag
+    pltpu.make_async_copy(last, last, recv_sem.at[len(GROUPS) - 1]).wait()
     @pl.when(tm < 3)
     def _():
         for halo in halos:
@@ -279,11 +302,12 @@
     table = jnp.asarray(tables(nfft, 4 * frames))
     vmem = pl.BlockSpec(memory_space=pltpu.VMEM)
     hbm = pl.BlockSpec(memory_space=pltpu.HBM)
-    return pl.pallas_call(
+    result = jax.ShapeDtypeStruct((2, 8, 256, 256), F32)
+    begun, last = pl.pallas_call(
         kernel,
-        out_shape=jax.ShapeDtypeStruct((2, 8, 256, 256), F32),
+        out_shape=(result, jax.ShapeDtypeStruct((1, 4, 256, LANES), F32)),
         in_specs=[hbm, hbm, hbm],
-        out_specs=vmem,
+        out_specs=(vmem, vmem),
         scratch_shapes=[
             pltpu.VMEM(taps.shape, F32),
             pltpu.VMEM(table.shape, BF16),
@@ -291,16 +315,24 @@
             pltpu.VMEM((4, nfft // LANES, 8, LANES), F32),
             pltpu.VMEM((9, 2, 3, inputs * frames, LANES), BF16),
             pltpu.VMEM((DEVICES, 8, inputs, LANES), F32),
-            pltpu.VMEM((8, 4, 256, LANES), F32),
+            pltpu.VMEM((7, 4, 256, LANES), F32),
             pltpu.SemaphoreType.DMA((nfft // LANES + 2,)),
             pltpu.SemaphoreType.DMA((nfft // LANES,)),
             pltpu.SemaphoreType.DMA((nfft // LANES,)),
-            pltpu.SemaphoreType.REGULAR((3,)),
+            pltpu.SemaphoreType.REGULAR,
             pltpu.SemaphoreType.DMA,
             pltpu.SemaphoreType.DMA((len(GROUPS),)),
         ],
         compiler_params=pltpu.CompilerParams(collective_id=0, has_side_effects=True, vmem_limit_bytes=40 << 20),
     )(*(pltpu.with_memory_space_constraint(v, pltpu.HBM) for v in (voltages, taps, table)))
+    return pl.pallas_call(
+        tail_kernel,
+        out_shape=result,
+        in_specs=[vmem, vmem],
+        out_specs=hbm,
+        scratch_shapes=[pltpu.VMEM((2, 256, 256), F32), pltpu.SemaphoreType.DMA((8,))],
+        compiler_params=pltpu.CompilerParams(vmem_limit_bytes=24 << 20),
+    )(begun, last)
 
 
 def solution(mesh):

time: 65.5 us -> 64.1 us (0.979)
  local copies, waits for them, and re-layouts: 2.02 us -> 0 us
    unnamed x1 -> x0, local copies, waits for them, and re-layouts: 2.02 us -> none
    pallas_call x1 -> x2, Pallas kernels: 63.4 us -> 64 us  [the longest x1 61.8 us: on_device(): pl.pallas_call(kernel, out_shape=(result, jax.ShapeDtypeStruct((1, 4, 256...]
where the time goes in v4:
time: 64.1 us; the launch traced here: 64 us
  Pallas kernels  64 us (100%)
    pallas_call x1, Pallas kernels, on_device(): pl.pallas_call(kernel, out_shape=(result, jax.ShapeDtypeStruct((1, 4, 256...  61.8 us
    pallas_call x1, Pallas kernels, on_device(): pl.pallas_call(tail_kernel, out_shape=result, in_specs=[vmem, vmem], out_...  2.24 us

profile of v4, /device:TPU:1, one launch (start us, length us, event | category | flops | bytes accessed | tf_op | source)
XLA Modules:
  0.0 64.0 jit_solution(7322386261727772409)
XLA Ops:
  0.0 61.8 %shard_map.37 = (f32[2,8,256,256]{3,2,1,0:T(8,128)S(1)}, f32[1,4,256,128]{3,2,1,0:T(8,128)S(1)}) custom-call(f32[8,64,2048]{2,1,0:T(8,128)} %volt.1, f32[4,2048]{1,0:T(4,128)} %taps_hbm.1, bf16[9,256,256]{2,1,0:T(8,128)(2,1)} %constant.2.clone.table_hbm), custom_call_target="tpu_custom_call" | custom-call | tf_op jit(solution)/shard_map/pallas_call | solution.py:306
  61.8 2.2 %shard_map.38 = f32[2,8,256,256]{3,2,1,0:T(8,128)} custom-call(f32[2,8,256,256]{3,2,1,0:T(8,128)S(1)} %get-tuple-element.7.begun, f32[1,4,256,128]{3,2,1,0:T(8,128)S(1)} %get-tuple-element.8.last), custom_call_target="tpu_custom_call" | custom-call | tf_op jit(solution)/shard_map/pallas_call | solution.py:328

commit v5 on v4

--- a/solution.py
+++ b/solution.py
@@ -68,7 +68,7 @@
 
 
 MESH = pl.DeviceIdType.MESH
-GROUPS = ((0, 2), (2, 2), (4, 2), (6, 1), (7, 1))
+GROUPS = ((1, 2), (3, 2), (5, 2), (7, 1), (0, 1))
 DEVICES = 128
 
 
@@ -98,16 +98,12 @@
 
 def tail_kernel(begun, last, out, stage, sem):
     tm = lax.axis_index("tm")
-    final = jnp.where(lax.rem(tm, 2) == 1, 1, 7)
-    writes = []
-    for k in range(1, 8):
-        chan = lax.rem(final + k, 8)
-        writes.append(pltpu.make_async_copy(begun.at[:, chan], out.at[:, chan], sem.at[k]))
-        writes[-1].start()
-    chan, real, imag = visibility([last[0, t] for t in range(4)], 7, tm)
+    writes = [pltpu.make_async_copy(begun.at[:, pl.ds(1, 7)], out.at[:, pl.ds(1, 7)], sem.at[0])]
+    writes[0].start()
+    _, real, imag = visibility([last[0, t] for t in range(4)], 0, tm)
     stage[0] = real
     stage[1] = imag
-    writes.append(pltpu.make_async_copy(stage, out.at[:, chan], sem.at[0]))
+    writes.append(pltpu.make_async_copy(stage, out.at[:, 0], sem.at[1]))
     writes[-1].start()
     for write in writes:
         write.wait()
@@ -220,7 +216,6 @@
         filtered(i, 0)
 
     loads[1].wait()
-    pl.semaphore_wait(column_sem, 7)
 
     def operand(r, part, pair):
         rows_ = []
@@ -249,7 +244,7 @@
     rows = pl.ds(pl.multiple_of(inp * 8, 8), 8)
 
     def landing(first, count):
-        return last.at[pl.ds(0, 1), tm, rows, :] if first == 7 else recv.at[pl.ds(first, count), tm, rows, :]
+        return last.at[pl.ds(0, 1), tm, rows, :] if first == 0 else recv.at[pl.ds(first - 1, count), tm, rows, :]
 
     def ship(g, to_inp, to_tm):
         first, count = GROUPS[g]
@@ -272,7 +267,12 @@
     def exchange(g):
         first, count = GROUPS[g]
         pltpu.make_async_copy(send.at[me, pl.ds(first, count)], landing(first, count), recv_sem.at[g]).start()
-        for dx, dy, dz, dc in offsets():
+        steps = offsets()
+        if g == 0:
+            steps = [step for step in steps if step[1] == step[3] == 0] + [step for step in steps if step[1] or step[3]]
+        for k, (dx, dy, dz, dc) in enumerate(steps):
+            if g == 0 and k == 15:
+                pl.semaphore_wait(column_sem, 7)
             ship(g, y_at[dy][0] + x_at[dx] + z_at[dz], y_at[dy][1] + core_at[dc])
 
     for g, (first, count) in enumerate(GROUPS):
@@ -281,10 +281,10 @@
         exchange(g)
 
     for g, (first, count) in enumerate(GROUPS[:-1]):
-        slots = recv.at[pl.ds(first, count)]
+        slots = recv.at[pl.ds(first - 1, count)]
         pltpu.make_async_copy(slots, slots, recv_sem.at[g]).wait()
         for r in range(first, first + count):
-            chan, real, imag = visibility([recv[r, t] for t in range(4)], r, tm)
+            chan, real, imag = visibility([recv[r - 1, t] for t in range(4)], r, tm)
             out[0, chan] = real
             out[1, chan] = imag
     pltpu.make_async_copy(last, last, recv_sem.at[len(GROUPS) - 1]).wait()
@@ -330,7 +330,7 @@
         out_shape=result,
         in_specs=[vmem, vmem],
         out_specs=hbm,
-        scratch_shapes=[pltpu.VMEM((2, 256, 256), F32), pltpu.SemaphoreType.DMA((8,))],
+        scratch_shapes=[pltpu.VMEM((2, 256, 256), F32), pltpu.SemaphoreType.DMA((2,))],
         compiler_params=pltpu.CompilerParams(vmem_limit_bytes=24 << 20),
     )(begun, last)
 

time: 64.1 us -> 63.8 us (level)
  no operation moved by 1% of the time
where the time goes in v5:
time: 63.8 us; the launch traced here: 63.7 us
  Pallas kernels  63.7 us (100%)
    pallas_call x1, Pallas kernels, on_device(): pl.pallas_call(kernel, out_shape=(result, jax.ShapeDtypeStruct((1, 4, 256...  61.7 us
    pallas_call x1, Pallas kernels, on_device(): pl.pallas_call(tail_kernel, out_shape=result, in_specs=[vmem, vmem], out_...  2.02 us

profile of v5, /device:TPU:1, one launch (start us, length us, event | category | flops | bytes accessed | tf_op | source)
XLA Modules:
  0.0 63.7 jit_solution(10037066323576733522)
XLA Ops:
  0.0 61.7 %shard_map.37 = (f32[2,8,256,256]{3,2,1,0:T(8,128)S(1)}, f32[1,4,256,128]{3,2,1,0:T(8,128)S(1)}) custom-call(f32[8,64,2048]{2,1,0:T(8,128)} %volt.1, f32[4,2048]{1,0:T(4,128)} %taps_hbm.1, bf16[9,256,256]{2,1,0:T(8,128)(2,1)} %constant.2.clone.table_hbm), custom_call_target="tpu_custom_call" | custom-call | tf_op jit(solution)/shard_map/pallas_call | solution.py:306
  61.7 2.0 %shard_map.38 = f32[2,8,256,256]{3,2,1,0:T(8,128)} custom-call(f32[2,8,256,256]{3,2,1,0:T(8,128)S(1)} %get-tuple-element.7.begun, f32[1,4,256,128]{3,2,1,0:T(8,128)S(1)} %get-tuple-element.8.last), custom_call_target="tpu_custom_call" | custom-call | tf_op jit(solution)/shard_map/pallas_call | solution.py:328

commit v6 on v5

--- a/solution.py
+++ b/solution.py
@@ -68,7 +68,7 @@
 
 
 MESH = pl.DeviceIdType.MESH
-GROUPS = ((1, 2), (3, 2), (5, 2), (7, 1), (0, 1))
+GROUPS = ((1, 1), (2, 2), (4, 2), (6, 2), (0, 1))
 DEVICES = 128
 
 

time: 63.8 us -> 63.2 us (level)
  no operation moved by 1% of the time
where the time goes in v6:
time: 63.2 us; the launch traced here: 63.1 us
  Pallas kernels  63.1 us (100%)
    pallas_call x1, Pallas kernels, on_device(): pl.pallas_call(kernel, out_shape=(result, jax.ShapeDtypeStruct((1, 4, 256...  61.1 us
    pallas_call x1, Pallas kernels, on_device(): pl.pallas_call(tail_kernel, out_shape=result, in_specs=[vmem, vmem], out_...  2.02 us

profile of v6, /device:TPU:1, one launch (start us, length us, event | category | flops | bytes accessed | tf_op | source)
XLA Modules:
  0.0 63.1 jit_solution(5949016065739279407)
XLA Ops:
  0.0 61.1 %shard_map.37 = (f32[2,8,256,256]{3,2,1,0:T(8,128)S(1)}, f32[1,4,256,128]{3,2,1,0:T(8,128)S(1)}) custom-call(f32[8,64,2048]{2,1,0:T(8,128)} %volt.1, f32[4,2048]{1,0:T(4,128)} %taps_hbm.1, bf16[9,256,256]{2,1,0:T(8,128)(2,1)} %constant.2.clone.table_hbm), custom_call_target="tpu_custom_call" | custom-call | tf_op jit(solution)/shard_map/pallas_call | solution.py:306
  61.1 2.0 %shard_map.38 = f32[2,8,256,256]{3,2,1,0:T(8,128)} custom-call(f32[2,8,256,256]{3,2,1,0:T(8,128)S(1)} %get-tuple-element.7.begun, f32[1,4,256,128]{3,2,1,0:T(8,128)S(1)} %get-tuple-element.8.last), custom_call_target="tpu_custom_call" | custom-call | tf_op jit(solution)/shard_map/pallas_call | solution.py:328

commit v7 on v6

--- a/solution.py
+++ b/solution.py
@@ -80,7 +80,13 @@
 def offsets():
     shuffled = np.random.RandomState(1).permutation(np.arange(1, DEVICES))
     steps = [(int(k) // 2 % 4, int(k) // 8 % 4, int(k) // 32, int(k) % 2) for k in shuffled]
-    return sorted(steps, key=lambda step: -sum(min(d, 4 - d) for d in step[:3]))
+    rank = {step: k for k, step in enumerate(steps)}
+
+    def order(step):
+        back = tuple((4 - d) % 4 for d in step[:3]) + step[3:]
+        return -sum(min(d, 4 - d) for d in step[:3]), min(rank[step], rank[back]), rank[step]
+
+    return sorted(steps, key=order)
 
 
 def visibility(blocks, r, tm):

time: 63.2 us -> 63 us (level)
  no operation moved by 1% of the time
where the time goes in v7:
time: 63 us; the launch traced here: 62.9 us
  Pallas kernels  62.8 us (100%)
    pallas_call x1, Pallas kernels, on_device(): pl.pallas_call(kernel, out_shape=(result, jax.ShapeDtypeStruct((1, 4, 256...  60.8 us
    pallas_call x1, Pallas kernels, on_device(): pl.pallas_call(tail_kernel, out_shape=result, in_specs=[vmem, vmem], out_...  2.02 us

profile of v7, /device:TPU:1, one launch (start us, length us, event | category | flops | bytes accessed | tf_op | source)
XLA Modules:
  0.0 62.9 jit_solution(5938819514858330674)
XLA Ops:
  0.0 60.8 %shard_map.37 = (f32[2,8,256,256]{3,2,1,0:T(8,128)S(1)}, f32[1,4,256,128]{3,2,1,0:T(8,128)S(1)}) custom-call(f32[8,64,2048]{2,1,0:T(8,128)} %volt.1, f32[4,2048]{1,0:T(4,128)} %taps_hbm.1, bf16[9,256,256]{2,1,0:T(8,128)(2,1)} %constant.2.clone.table_hbm), custom_call_target="tpu_custom_call" | custom-call | tf_op jit(solution)/shard_map/pallas_call | solution.py:312
  60.8 2.0 %shard_map.38 = f32[2,8,256,256]{3,2,1,0:T(8,128)} custom-call(f32[2,8,256,256]{3,2,1,0:T(8,128)S(1)} %get-tuple-element.7.begun, f32[1,4,256,128]{3,2,1,0:T(8,128)S(1)} %get-tuple-element.8.last), custom_call_target="tpu_custom_call" | custom-call | tf_op jit(solution)/shard_map/pallas_call | solution.py:334
